TPU v7x, 512 devices: a whole 4x8x8 slice. The times are simulated.
512 devices in a mesh: band: 8 (over y), gy: 8 (over z), gz: 8 (over x, core).
Axes of the slice: x: 4, y: 8, z: 8, core: 2. Of those that a mesh axis runs over, the one named last changes fastest.
Arguments:
- orbitals: float32 [1024, 48, 3840], P('band', 'gy', 'gz'), may hold values from -6 to 6
- occupied: bfloat16 [1024, 48, 3840], P('band', 'gy', 'gz'), may hold values from -6 to 6
- eigen: float32 [1024], P('band'), may hold values from -1.5 to 0
- potential: float32 [48, 3840], P('gy', 'gz'), may hold values from -2 to 0.5
- perturbation: float32 [48, 3840], P('gy', 'gz'), may hold values from 0.2 to 1.5
- precondition: float32 [48, 3840], P('gy', 'gz'), may hold values from 0.05 to 0.3
Outputs:
- updated: float32 [1024, 48, 3840], P('band', 'gy', 'gz')
- resid_norm: float32 [1024], P('band')
All inputs are finite; a program needn't handle non-finite values.
Results may differ from a plain program's by a relative error of at most 0.0008.
Values may be sent and summed in bfloat16 or wider, within the bound.
A program may use at most 128 MiB of HBM per device.

v0:
```python
import jax
import jax.numpy as jnp
from jax import lax
from jax.sharding import PartitionSpec as P

NX = 80
stencil = (-205.0 / 72.0, 8.0 / 5.0, -1.0 / 5.0, 8.0 / 315.0, -1.0 / 560.0)


def extended(block, sides, width):
    for axis, dim in sides:
        count = lax.axis_size(axis)
        forward = [(i, i + 1) for i in range(count - 1)]
        forward.append((count - 1, 0))
        backward = [(target, source) for source, target in forward]
        low = lax.ppermute(
            lax.slice_in_dim(block, block.shape[dim] - width, None, axis=dim), axis, forward
        )
        high = lax.ppermute(lax.slice_in_dim(block, 0, width, axis=dim), axis, backward)
        block = jnp.concatenate([low, block, high], axis=dim)
    return block


def along_x(field, dist):
    flat = field.shape[-1]
    position = lax.broadcasted_iota(jnp.int32, (flat,), 0) % NX
    lower = jnp.where(position >= dist, jnp.roll(field, dist, -1), jnp.roll(field, dist - NX, -1))
    upper = jnp.where(
        position < NX - dist, jnp.roll(field, -dist, -1), jnp.roll(field, NX - dist, -1)
    )
    return lower + upper


def laplace(field):
    rows_y = field.shape[1]
    flat = field.shape[2]
    padded_y = extended(field, (("gy", 1),), 4)
    padded_z = extended(field, (("gz", 2),), 4 * NX)
    total = 3.0 * stencil[0] * field
    for dist in range(1, 5):
        pair_y = (
            padded_y[:, 4 + dist : 4 + dist + rows_y, :]
            + padded_y[:, 4 - dist : 4 - dist + rows_y, :]
        )
        pair_z = (
            padded_z[:, :, (4 + dist) * NX : (4 + dist) * NX + flat]
            + padded_z[:, :, (4 - dist) * NX : (4 - dist) * NX + flat]
        )
        total = total + stencil[dist] * (along_x(field, dist) + pair_y + pair_z)
    return total


def on_device(orbitals, occupied, eigen, potential, perturbation, precondition):
    band_rows, rows_y, flat = orbitals.shape
    cells = NX * rows_y * lax.axis_size("gy") * (flat // NX) * lax.axis_size("gz")
    occ_wide = occupied.astype(jnp.float32)
    resid = (
        -0.5 * laplace(orbitals)
        + (potential[None] - eigen[:, None, None]) * orbitals
        + perturbation[None] * occ_wide
    )
    squares = jnp.sum(resid * resid, axis=(1, 2))
    squares = lax.psum(squares, ("gy", "gz"))
    trial = orbitals - precondition[None] * resid
    trial_low = trial.astype(jnp.bfloat16)
    partial_margins = jnp.einsum(
        "oyc,ryc->or",
        lax.all_gather(occupied, "band", axis=0, tiled=True),
        trial_low,
        preferred_element_type=jnp.float32,
    )
    margins = lax.psum(partial_margins, ("gy", "gz"))
    norms = jnp.sqrt(squares / cells + 1e-06)
    coeff = (margins / cells).astype(jnp.bfloat16)
    correction = jnp.einsum(
        "or,oyc->ryc",
        coeff,
        lax.all_gather(occupied, "band", axis=0, tiled=True),
        preferred_element_type=jnp.float32,
    )
    updated = trial - correction
    return (updated, norms)


def solution(mesh):
    placed = (
        P("band", "gy", "gz"),
        P("band", "gy", "gz"),
        P("band"),
        P("gy", "gz"),
        P("gy", "gz"),
        P("gy", "gz"),
    )
    return jax.shard_map(
        on_device,
        mesh=mesh,
        in_specs=placed,
        out_specs=(P("band", "gy", "gz"), P("band")),
        check_vma=False,
    )
```

profile of v0, /device:TPU:8, one launch (start us, length us, event | category | flops | bytes accessed | tf_op | source)
XLA Modules:
  0.0 306.1 jit_solution(4770405374905059568)
XLA Ops:
  7.2 0.7 all-gather.2.cloned.1.call-update
  8.0 1.7 fusion.56
  9.7 4.3 %collective-permute-start.1 = (f32[128,4,480]{0,2,1:T(8,128)S(1)}, f32[128,4,480]{0,2,1:T(8,128)S(1)}, u32[]{:S(2)}, u32[]{:S(2)}) collective-permute-start(f32[128,4,480]{0,2,1:T(8,128)S(1)} %get-tuple-element.37), channel_id=1, source_target_pairs={{0,8},{8,16},{16,24},{24,32},{32,40},{40,48},{48,56},{56,0},{1,9},... | collective-permute-start | bytes 2949128 | tf_op jit(solution)/shard_map/ppermute | solution.py:16
  14.2 8.6 %collective-permute-start = (f32[128,4,480]{0,2,1:T(8,128)S(1)}, f32[128,4,480]{0,2,1:T(8,128)S(1)}, u32[]{:S(2)}, u32[]{:S(2)}) collective-permute-start(f32[128,4,480]{0,2,1:T(8,128)S(1)} %get-tuple-element.36), channel_id=1, source_target_pairs={{8,0},{16,8},{24,16},{32,24},{40,32},{48,40},{56,48},{0,56},{9,1},... | collective-permute-start | bytes 2949128 | tf_op jit(solution)/shard_map/ppermute | solution.py:19
  22.8 2.7 collective-permute-start.2
  26.1 0.8 fusion.47
  27.0 0.8 fusion.51
  27.8 0.9 fusion.55
  28.7 1.2 fusion.46
  29.9 1.6 fusion.50
  31.5 1.9 fusion.45
  33.4 1.9 fusion.49
  35.3 1.8 fusion.53
  37.1 1.8 fusion.41
  40.0 1.6 fusion.54
  42.7 1.6 fusion.42
  44.5 0.6 constant_dynamic-update-slice_fusion.1
  45.4 0.6 copy-done.2
  46.0 13.7 %multiply_reduce_fusion = (f32[128]{0:T(128)}, f32[128,6,480]{0,2,1:T(8,128)S(1)}) fusion(bf16[128,6,480]{0,2,1:T(8,128)(2,1)} %param.7, f32[6,480]{1,0:T(8,128)S(1)} %copy-done.2, f32[128,6,480]{0,2,1:T(8,128)S(1)} %copy-done, f32[128]{0:T(128)} %param.8, f32[6,480]{1,0:T(8,128)S(1)} %copy-done.3, f32[128,6,800]{0,2,1:T(8,128)S(1)} %get-tuple-element.39, ...), kind=kLoop, calls=%fused_computation.39 | loop fusion | flops 22855552 | bytes 50900224 | tf_op jit(solution)/shard_map/reduce_sum | solution.py:62
  59.7 35.2 %all-gather.2.cloned.1.call-done = bf16[1024,6,480]{0,2,1:T(8,128)(2,1)} async-done(((bf16[128,6,480]{0,2,1:T(8,128)(2,1)}), bf16[1024,6,480]{0,2,1:T(8,128)(2,1)}) %all-gather.2.cloned.1.call-update) | async-done | bytes 5898256 | tf_op jit(solution)/shard_map/all_gather | solution.py:68
  94.9 6.2 %convolution_bitcast_fusion = f32[1024,128]{1,0:T(8,128)} fusion(bf16[1024,6,480]{0,2,1:T(8,128)(2,1)} %all-gather.2.cloned.1.call-done, f32[128,6,480]{0,2,1:T(8,128)S(1)} %copy-done, f32[128,6,480]{0,2,1:T(8,128)S(1)} %get-tuple-element.3, f32[6,480]{1,0:T(8,128)S(1)} %copy-done.1), kind=kOutput, calls=%fused_computation.42 | convolution fusion | flops 756080640 | bytes 9383168 | tf_op jit(solution)/shard_map/oyc,ryc->or/dot_general | solution.py:66
  101.1 125.7 %psum.15 = f32[128]{0:T(128)S(1)} all-reduce(f32[128]{0:T(128)S(1)} %copy-done.4), channel_id=1, replica_groups=mesh['band'=8,'gy'=8,'gz'=8] {'gy','gz'}, use_global_device_ids=true, to_apply=%region_2.3 | all-reduce | flops 128 | bytes 1024 | tf_op jit(solution)/shard_map/psum | solution.py:63
  227.3 66.2 %all-reduce.2.cloned.1.call-done = f32[1024,128]{1,0:T(8,128)} async-done(((f32[1024,128]{1,0:T(8,128)}), f32[1024,128]{1,0:T(8,128)}) %all-reduce.2.cloned.1.call-update) | async-done | bytes 524304 | tf_op jit(solution)/shard_map/psum | solution.py:72
  293.6 5.7 %convolution_subtract_fusion = f32[128,6,480]{0,2,1:T(8,128)} fusion(bf16[1024,6,480]{0,2,1:T(8,128)(2,1)} %all-gather.2.cloned.1.call-done, f32[128,6,480]{0,2,1:T(8,128)S(1)} %copy-done, f32[128,6,480]{0,2,1:T(8,128)S(1)} %get-tuple-element.3, f32[6,480]{1,0:T(8,128)S(1)} %copy-done.1, f32[1024,128]{1,0:T(8,128)} %all-reduce.2.cloned.1.call-done), kind=kOutput, calls=%fused_computation.41 | convolution fusion | flops 756342784 | bytes 10857728 | tf_op jit(solution)/shard_map/or,oyc->ryc/dot_general | solution.py:75
  (32 shorter events, 4.0 us)
Async XLA Ops:
  7.2 87.7 %all-gather.2.cloned.1.call-start = ((), (), s32[]{:S(2)}) async-start(), calls=%async_computation | async-start | bytes 6635520 | tf_op jit(solution)/shard_map/all_gather | solution.py:68
  7.9 6.1 %copy-start = (f32[128,6,480]{0,2,1:T(8,128)S(1)}, f32[128,6,480]{0,2,1:T(8,128)}, u32[]{:S(2)}) copy-start(f32[128,6,480]{0,2,1:T(8,128)} %param.6) | copy-start | bytes 4423684
  7.9 285.7 %all-reduce.2.cloned.1.call-start = ((), (), s32[]{:S(2)}) async-start(), calls=%async_computation.1 | async-start | bytes 1048576 | tf_op jit(solution)/shard_map/psum | solution.py:72
  9.7 34.7 %collective-permute-start.1 = (f32[128,4,480]{0,2,1:T(8,128)S(1)}, f32[128,4,480]{0,2,1:T(8,128)S(1)}, u32[]{:S(2)}, u32[]{:S(2)}) collective-permute-start(f32[128,4,480]{0,2,1:T(8,128)S(1)} %get-tuple-element.37), channel_id=1, source_target_pairs={{0,8},{8,16},{16,24},{24,32},{32,40},{40,48},{48,56},{56,0},{1,9},... | collective-permute-start | bytes 2949128 | tf_op jit(solution)/shard_map/ppermute | solution.py:16
  14.2 30.3 %collective-permute-start.3 = (f32[128,6,320]{0,2,1:T(8,128)S(1)}, f32[128,6,320]{0,2,1:T(8,128)S(1)}, u32[]{:S(2)}, u32[]{:S(2)}) collective-permute-start(f32[128,6,320]{0,2,1:T(8,128)S(1)} %get-tuple-element.43), channel_id=1, source_target_pairs={{0,1},{1,2},{2,3},{3,4},{4,5},{5,6},{6,7},{7,0},{8,9},{9,10},{10,1... | collective-permute-start | bytes 2949128 | tf_op jit(solution)/shard_map/ppermute | solution.py:16
  14.2 31.0 %collective-permute-start = (f32[128,4,480]{0,2,1:T(8,128)S(1)}, f32[128,4,480]{0,2,1:T(8,128)S(1)}, u32[]{:S(2)}, u32[]{:S(2)}) collective-permute-start(f32[128,4,480]{0,2,1:T(8,128)S(1)} %get-tuple-element.36), channel_id=1, source_target_pairs={{8,0},{16,8},{24,16},{32,24},{40,32},{48,40},{56,48},{0,56},{9,1},... | collective-permute-start | bytes 2949128 | tf_op jit(solution)/shard_map/ppermute | solution.py:19
  22.8 22.5 %collective-permute-start.2 = (f32[128,6,320]{0,2,1:T(8,128)S(1)}, f32[128,6,320]{0,2,1:T(8,128)S(1)}, u32[]{:S(2)}, u32[]{:S(2)}) collective-permute-start(f32[128,6,320]{0,2,1:T(8,128)S(1)} %get-tuple-element.42), channel_id=1, source_target_pairs={{1,0},{2,1},{3,2},{4,3},{5,4},{6,5},{7,6},{0,7},{9,8},{10,9},{11,1... | collective-permute-start | bytes 2949128 | tf_op jit(solution)/shard_map/ppermute | solution.py:19
  45.2 0.7 copy-start.2
  45.3 0.7 copy-start.3
  46.0 48.9 %copy-start.1 = (f32[6,480]{1,0:T(8,128)S(1)}, f32[6,480]{1,0:T(8,128)}, u32[]{:S(2)}) copy-start(f32[6,480]{1,0:T(8,128)} %param.11) | copy-start | bytes 34564
  94.9 6.3 %copy-start.4 = (f32[128]{0:T(128)S(1)}, f32[128]{0:T(128)}, u32[]{:S(2)}) copy-start(f32[128]{0:T(128)} %get-tuple-element.2) | copy-start | bytes 1540
Sparse Core Ops, SparseCore 0:
  10.0 84.8 all-gather.1
  101.2 192.2 all-reduce.1
where the time goes:
time: 306 us
  blocking collectives  126 us (41%)
  waiting for transfers between devices  102 us (33%)
  local copies, waits for them, and re-layouts  20.1 us (7%)
  other arithmetic  16.5 us (5%)
  starting transfers between devices  15.6 us (5%)
  between operations  14.2 us (5%)
  matrix products  11.9 us (4%)
    psum x1, blocking collectives, on_device(): squares = lax.psum(squares, ('gy', 'gz'))  126 us
    psum x1, waiting for transfers between devices, on_device(): margins = lax.psum(partial_margins, ('gy', 'gz'))  66.2 us
    all_gather x1, waiting for transfers between devices, on_device(): lax.all_gather(occupied, 'band', axis=0, tiled=True)  35.2 us
    reduce_sum x1, other arithmetic, on_device(): squares = jnp.sum(resid * resid, axis=(1, 2))  13.7 us
    ppermute x2, starting transfers between devices, extended(): lax.ppermute(lax.slice_in_dim(block, 0, width, axis=dim), axis, backward)  11.2 us
    slice x8, local copies, waits for them, and re-layouts, along_x(): jnp.roll(field, dist - NX, -1)  8.63 us
    slice x8, local copies, waits for them, and re-layouts, along_x(): jnp.roll(field, dist, -1)  8.03 us
    dot_general x1, matrix products, on_device(): jnp.einsum('oyc,ryc->or', lax.all_gather(occupied, 'band', axis=0, tiled=...  6.24 us
  transfers between devices with their start and end apart: 6, of which 2 were waited for; matrix products, arithmetic and copies ran while one was open for 12% of the time, Pallas kernels for 0%

commit v1 on v0

--- a/solution.py
+++ b/solution.py
@@ -2,6 +2,7 @@
 import jax.numpy as jnp
 from jax import lax
 from jax.sharding import PartitionSpec as P
+from jax.lax import axis_index, ppermute, psum
 
 NX = 80
 stencil = (-205.0 / 72.0, 8.0 / 5.0, -1.0 / 5.0, 8.0 / 315.0, -1.0 / 560.0)
@@ -63,11 +64,52 @@
     squares = lax.psum(squares, ("gy", "gz"))
     trial = orbitals - precondition[None] * resid
     trial_low = trial.astype(jnp.bfloat16)
-    partial_margins = jnp.einsum(
-        "oyc,ryc->or",
-        lax.all_gather(occupied, "band", axis=0, tiled=True),
-        trial_low,
-        preferred_element_type=jnp.float32,
+
+    def store_spans(values, axis_id, state):
+        value_now = psum(1, axis_name=axis_id)
+        x_next = axis_index(axis_id)
+        w1, q_next, odd = (value_now, x_next, values.shape[0])
+        buffers = []
+        w = 0
+        while w < w1:
+            buffers.append((w, (w + 1) % w1))
+            w += 1
+        ledger = []
+        for rr, j0 in buffers:
+            ledger.append((j0, rr))
+        view_out = ppermute(values, axis_name=axis_id, perm=buffers)
+        base_arr = ppermute(values, axis_name=axis_id, perm=ledger)
+        part_now, current_block = (view_out, base_arr)
+        w_next = state(values, q_next * odd)
+        step_out = w_next.shape[0]
+        later = jnp.zeros((*w_next.shape[:0], w1 * step_out, *w_next.shape[1:]), w_next.dtype)
+
+        def modes_plan(later, w_next, y1):
+            return lax.dynamic_update_slice_in_dim(later, w_next, y1 * step_out, axis=0)
+
+        later = modes_plan(later, w_next, q_next)
+        u = 1
+        while u < w1 // 2 + 1:
+            e_now, local_part = ((q_next - u) % w1, (q_next + u) % w1)
+            small = (part_now, current_block)
+            if u < w1 // 2:
+                answer = ppermute(part_now, axis_name=axis_id, perm=buffers)
+                prior = ppermute(current_block, axis_name=axis_id, perm=ledger)
+                part_now, current_block = (answer, prior)
+            f_now = state(small[0], e_now * odd)
+            later = modes_plan(later, f_now, e_now)
+            if 2 * u < w1:
+                w2 = state(small[1], local_part * odd)
+                later = modes_plan(later, w2, local_part)
+            u = u + 1
+        return later
+
+    partial_margins = store_spans(
+        occupied,
+        "band",
+        lambda shard, offset: jnp.einsum(
+            "oyc,ryc->or", shard, trial_low, preferred_element_type=jnp.float32
+        ),
     )
     margins = lax.psum(partial_margins, ("gy", "gz"))
     norms = jnp.sqrt(squares / cells + 1e-06)

time: 306 us -> 329 us (1.075)
  starting transfers between devices: 15.6 us -> 37.6 us
  waiting for transfers between devices: 102 us -> 93.7 us
  local copies, waits for them, and re-layouts: 20.1 us -> 24.9 us
    all_gather x1, waiting for transfers between devices: 35.2 us -> 0.01 us  [on_device(): lax.all_gather(occupied, 'band', axis=0, tiled=True)]
    ppermute x0 -> x7, starting transfers between devices: none -> 25.8 us  [the longest x3 10.5 us: store_spans(): answer = ppermute(part_now, axis_name=axis_id, perm=buffers)]
    ppermute x0 -> x7, waiting for transfers between devices: none -> 24.5 us  [the longest x3 23 us: store_spans(): answer = ppermute(part_now, axis_name=axis_id, perm=buffers)]
    dot_general x1 -> x8, matrix products: 6.24 us -> 8 us  [on_device(): jnp.einsum('oyc,ryc->or', shard, trial_low, preferred_element_type=jnp.fl...]
  transfers between devices with their start and end apart: 6 -> 13, of which waited for: 2 -> 5; matrix products, arithmetic and copies ran while one was open for 12% -> 14% of each run, Pallas kernels for 0% -> 0%
where the time goes in v1:
time: 329 us
  blocking collectives  129 us (39%)
  waiting for transfers between devices  93.7 us (28%)
  starting transfers between devices  37.6 us (11%)
  local copies, waits for them, and re-layouts  24.9 us (8%)
  between operations  16 us (5%)
  other arithmetic  14.3 us (4%)
  matrix products  13.7 us (4%)
    psum x1, blocking collectives, on_device(): squares = lax.psum(squares, ('gy', 'gz'))  129 us
    psum x1, waiting for transfers between devices, on_device(): margins = lax.psum(partial_margins, ('gy', 'gz'))  67.5 us
    ppermute x3, waiting for transfers between devices, store_spans(): answer = ppermute(part_now, axis_name=axis_id, perm=buffers)  23 us
    reduce_sum x1, other arithmetic, on_device(): squares = jnp.sum(resid * resid, axis=(1, 2))  13.3 us
    ppermute x3, starting transfers between devices, store_spans(): answer = ppermute(part_now, axis_name=axis_id, perm=buffers)  10.5 us
    ppermute x2, starting transfers between devices, extended(): lax.ppermute(lax.slice_in_dim(block, 0, width, axis=dim), axis, backward)  9.81 us
    slice x8, local copies, waits for them, and re-layouts, along_x(): jnp.roll(field, dist - NX, -1)  8.95 us
    dot_general x8, matrix products, on_device(): jnp.einsum('oyc,ryc->or', shard, trial_low, preferred_element_type=jnp.fl...  8 us
  transfers between devices with their start and end apart: 13, of which 5 were waited for; matrix products, arithmetic and copies ran while one was open for 14% of the time, Pallas kernels for 0%

profile of v1, /device:TPU:8, one launch (start us, length us, event | category | flops | bytes accessed | tf_op | source)
XLA Modules:
  0.0 328.7 jit_solution(14691329094101569301)
XLA Ops:
  8.1 3.6 %collective-permute-start.4 = (bf16[128,6,480]{0,2,1:T(8,128)(2,1)}, bf16[128,6,480]{0,2,1:T(8,128)(2,1)}, u32[]{:S(2)}, u32[]{:S(2)}) collective-permute-start(bf16[128,6,480]{0,2,1:T(8,128)(2,1)} %param.7), channel_id=1, source_target_pairs={{0,64},{64,128},{128,192},{192,256},{256,320},{320,384},{384,448},... | collective-permute-start | bytes 2211848 | tf_op jit(solution)/shard_map/ppermute | solution.py:80
  11.7 6.2 %collective-permute-start.5 = (bf16[128,6,480]{0,2,1:T(8,128)(2,1)}, bf16[128,6,480]{0,2,1:T(8,128)(2,1)}, u32[]{:S(2)}, u32[]{:S(2)}) collective-permute-start(bf16[128,6,480]{0,2,1:T(8,128)(2,1)} %param.7), channel_id=1, source_target_pairs={{64,0},{128,64},{192,128},{256,192},{320,256},{384,320},{448,384},... | collective-permute-start | bytes 2211848 | tf_op jit(solution)/shard_map/ppermute | solution.py:81
  17.9 3.0 fusion.64
  20.8 1.9 collective-permute-start.1
  24.2 7.1 %collective-permute-start = (f32[128,4,480]{0,2,1:T(8,128)}, f32[128,4,480]{0,2,1:T(8,128)S(1)}, u32[]{:S(2)}, u32[]{:S(2)}) collective-permute-start(f32[128,4,480]{0,2,1:T(8,128)} %get-tuple-element.36), channel_id=1, source_target_pairs={{8,0},{16,8},{24,16},{32,24},{40,32},{48,40},{56,48},{0,56},{9,1},... | collective-permute-start | bytes 2949128 | tf_op jit(solution)/shard_map/ppermute | solution.py:20
  31.4 1.8 fusion.53
  33.2 1.8 fusion.57
  35.0 1.8 fusion.61
  36.8 1.9 fusion.49
  38.7 1.6 fusion.54
  40.3 1.6 fusion.58
  41.9 1.7 fusion.62
  46.3 2.7 collective-permute-start.2
  50.6 3.5 %collective-permute-start.6 = (bf16[128,6,480]{0,2,1:T(8,128)(2,1)}, bf16[128,6,480]{0,2,1:T(8,128)(2,1)}, u32[]{:S(2)}, u32[]{:S(2)}) collective-permute-start(bf16[128,6,480]{0,2,1:T(8,128)(2,1)} %collective-permute-done.4), channel_id=1, source_target_pairs={{0,64},{64,128},{128,192},{192,256},{256,320},{320,384},{384,448},... | collective-permute-start | bytes 2211848 | tf_op jit(solution)/shard_map/ppermute | solution.py:96
  54.1 2.4 collective-permute-start.7
  61.1 13.3 %multiply_reduce_fusion = (f32[128]{0:T(128)}, f32[128,6,480]{0,2,1:T(8,128)S(1)}) fusion(bf16[128,6,480]{0,2,1:T(8,128)(2,1)S(1)} %copy-done.1, f32[6,480]{1,0:T(8,128)S(1)} %copy-done.6, f32[128,6,480]{0,2,1:T(8,128)S(1)} %copy-done, f32[128]{0:T(128)S(1)} %copy-done.8, f32[6,480]{1,0:T(8,128)S(1)} %copy-done.7, f32[128,6,800]{0,2,1:T(8,128)S(1)} %get-tuple-element.39, ...), kind=kLoop, calls=%fused_computation.39 | loop fusion | flops 22855552 | bytes 50900224 | tf_op jit(solution)/shard_map/reduce_sum | solution.py:63
  75.3 3.7 %collective-permute-start.8 = (bf16[128,6,480]{0,2,1:T(8,128)(2,1)}, bf16[128,6,480]{0,2,1:T(8,128)(2,1)S(1)}, u32[]{:S(2)}, u32[]{:S(2)}) collective-permute-start(bf16[128,6,480]{0,2,1:T(8,128)(2,1)} %collective-permute-done.6), channel_id=1, source_target_pairs={{0,64},{64,128},{128,192},{192,256},{256,320},{320,384},{384,448},... | collective-permute-start | bytes 2211848 | tf_op jit(solution)/shard_map/ppermute | solution.py:96
  82.2 3.1 collective-permute-start.9
  86.9 9.9 %collective-permute-done.8 = bf16[128,6,480]{0,2,1:T(8,128)(2,1)S(1)} collective-permute-done((bf16[128,6,480]{0,2,1:T(8,128)(2,1)}, bf16[128,6,480]{0,2,1:T(8,128)(2,1)S(1)}, u32[]{:S(2)}, u32[]{:S(2)}) %collective-permute-start.8) | collective-permute-done | bytes 737312 | tf_op jit(solution)/shard_map/ppermute | solution.py:96
  96.8 3.3 %collective-permute-start.10 = (bf16[128,6,480]{0,2,1:T(8,128)(2,1)S(1)}, bf16[128,6,480]{0,2,1:T(8,128)(2,1)S(1)}, u32[]{:S(2)}, u32[]{:S(2)}) collective-permute-start(bf16[128,6,480]{0,2,1:T(8,128)(2,1)S(1)} %collective-permute-done.8), channel_id=1, source_target_pairs={{0,64},{64,128},{128,192},{192,256},{256,320},{320,384},{384,448},... | collective-permute-start | bytes 2211848 | tf_op jit(solution)/shard_map/ppermute | solution.py:96
  104.1 13.1 %collective-permute-done.10 = bf16[128,6,480]{0,2,1:T(8,128)(2,1)S(1)} collective-permute-done((bf16[128,6,480]{0,2,1:T(8,128)(2,1)S(1)}, bf16[128,6,480]{0,2,1:T(8,128)(2,1)S(1)}, u32[]{:S(2)}, u32[]{:S(2)}) %collective-permute-start.10) | collective-permute-done | bytes 737312 | tf_op jit(solution)/shard_map/ppermute | solution.py:96
  119.0 128.6 %psum.15 = f32[128]{0:T(128)S(1)} all-reduce(f32[128]{0:T(128)S(1)} %copy-done.9), channel_id=1, replica_groups=mesh['band'=8,'gy'=8,'gz'=8] {'gy','gz'}, use_global_device_ids=true, to_apply=%region_2.3 | all-reduce | flops 128 | bytes 1024 | tf_op jit(solution)/shard_map/psum | solution.py:64
  248.1 67.5 %all-reduce.2.cloned.1.call-done = f32[1024,128]{1,0:T(8,128)} async-done(((f32[1024,128]{1,0:T(8,128)}), f32[1024,128]{1,0:T(8,128)}) %all-reduce.2.cloned.1.call-update) | async-done | bytes 524304 | tf_op jit(solution)/shard_map/psum | solution.py:114
  315.6 5.7 %convolution_subtract_fusion = f32[128,6,480]{0,2,1:T(8,128)} fusion(bf16[1024,6,480]{0,2,1:T(8,128)(2,1)} %all-gather.2.cloned.1.call-done, f32[128,6,480]{0,2,1:T(8,128)S(1)} %copy-done, f32[128,6,480]{0,2,1:T(8,128)S(1)} %get-tuple-element.3, f32[6,480]{1,0:T(8,128)S(1)} %copy-done.5, f32[1024,128]{1,0:T(8,128)} %all-reduce.2.cloned.1.call-done), kind=kOutput, calls=%fused_computation.41 | convolution fusion | flops 756342784 | bytes 10857728 | tf_op jit(solution)/shard_map/or,oyc->ryc/dot_general | solution.py:117
  (65 shorter events, 22.1 us)
Async XLA Ops:
  8.0 14.7 %copy-start = (f32[128,6,480]{0,2,1:T(8,128)S(1)}, f32[128,6,480]{0,2,1:T(8,128)}, u32[]{:S(2)}) copy-start(f32[128,6,480]{0,2,1:T(8,128)} %param.6) | copy-start | bytes 4423684
  8.0 307.6 %all-reduce.2.cloned.1.call-start = ((), (), s32[]{:S(2)}) async-start(), calls=%async_computation | async-start | bytes 1048576 | tf_op jit(solution)/shard_map/psum | solution.py:114
  8.1 38.3 %collective-permute-start.4 = (bf16[128,6,480]{0,2,1:T(8,128)(2,1)}, bf16[128,6,480]{0,2,1:T(8,128)(2,1)}, u32[]{:S(2)}, u32[]{:S(2)}) collective-permute-start(bf16[128,6,480]{0,2,1:T(8,128)(2,1)} %param.7), channel_id=1, source_target_pairs={{0,64},{64,128},{128,192},{192,256},{256,320},{320,384},{384,448},... | collective-permute-start | bytes 2211848 | tf_op jit(solution)/shard_map/ppermute | solution.py:80
  11.7 38.9 %collective-permute-start.5 = (bf16[128,6,480]{0,2,1:T(8,128)(2,1)}, bf16[128,6,480]{0,2,1:T(8,128)(2,1)}, u32[]{:S(2)}, u32[]{:S(2)}) collective-permute-start(bf16[128,6,480]{0,2,1:T(8,128)(2,1)} %param.7), channel_id=1, source_target_pairs={{64,0},{128,64},{192,128},{256,192},{320,256},{384,320},{448,384},... | collective-permute-start | bytes 2211848 | tf_op jit(solution)/shard_map/ppermute | solution.py:81
  20.8 33.3 %collective-permute-start.1 = (f32[128,4,480]{0,2,1:T(8,128)}, f32[128,4,480]{0,2,1:T(8,128)}, u32[]{:S(2)}, u32[]{:S(2)}) collective-permute-start(f32[128,4,480]{0,2,1:T(8,128)} %get-tuple-element.37), channel_id=1, source_target_pairs={{0,8},{8,16},{16,24},{24,32},{32,40},{40,48},{48,56},{56,0},{1,9},... | collective-permute-start | bytes 2949128 | tf_op jit(solution)/shard_map/ppermute | solution.py:17
  24.2 33.5 %collective-permute-start.3 = (f32[128,6,320]{0,2,1:T(8,128)}, f32[128,6,320]{0,2,1:T(8,128)}, u32[]{:S(2)}, u32[]{:S(2)}) collective-permute-start(f32[128,6,320]{0,2,1:T(8,128)} %get-tuple-element.43), channel_id=1, source_target_pairs={{0,1},{1,2},{2,3},{3,4},{4,5},{5,6},{6,7},{7,0},{8,9},{9,10},{10,1... | collective-permute-start | bytes 2949128 | tf_op jit(solution)/shard_map/ppermute | solution.py:17
  24.2 35.4 %collective-permute-start = (f32[128,4,480]{0,2,1:T(8,128)}, f32[128,4,480]{0,2,1:T(8,128)S(1)}, u32[]{:S(2)}, u32[]{:S(2)}) collective-permute-start(f32[128,4,480]{0,2,1:T(8,128)} %get-tuple-element.36), channel_id=1, source_target_pairs={{8,0},{16,8},{24,16},{32,24},{40,32},{48,40},{56,48},{0,56},{9,1},... | collective-permute-start | bytes 2949128 | tf_op jit(solution)/shard_map/ppermute | solution.py:20
  46.3 14.6 %collective-permute-start.2 = (f32[128,6,320]{0,2,1:T(8,128)}, f32[128,6,320]{0,2,1:T(8,128)S(1)}, u32[]{:S(2)}, u32[]{:S(2)}) collective-permute-start(f32[128,6,320]{0,2,1:T(8,128)} %get-tuple-element.42), channel_id=1, source_target_pairs={{1,0},{2,1},{3,2},{4,3},{5,4},{6,5},{7,6},{0,7},{9,8},{10,9},{11,1... | collective-permute-start | bytes 2949128 | tf_op jit(solution)/shard_map/ppermute | solution.py:20
  50.6 24.7 %collective-permute-start.6 = (bf16[128,6,480]{0,2,1:T(8,128)(2,1)}, bf16[128,6,480]{0,2,1:T(8,128)(2,1)}, u32[]{:S(2)}, u32[]{:S(2)}) collective-permute-start(bf16[128,6,480]{0,2,1:T(8,128)(2,1)} %collective-permute-done.4), channel_id=1, source_target_pairs={{0,64},{64,128},{128,192},{192,256},{256,320},{320,384},{384,448},... | collective-permute-start | bytes 2211848 | tf_op jit(solution)/shard_map/ppermute | solution.py:96
  54.1 28.1 %collective-permute-start.7 = (bf16[128,6,480]{0,2,1:T(8,128)(2,1)}, bf16[128,6,480]{0,2,1:T(8,128)(2,1)}, u32[]{:S(2)}, u32[]{:S(2)}) collective-permute-start(bf16[128,6,480]{0,2,1:T(8,128)(2,1)} %collective-permute-done.5), channel_id=1, source_target_pairs={{64,0},{128,64},{192,128},{256,192},{320,256},{384,320},{448,384},... | collective-permute-start | bytes 2211848 | tf_op jit(solution)/shard_map/ppermute | solution.py:97
  59.7 1.3 copy-start.1
  59.7 1.3 copy-start.3
  59.7 1.3 copy-start.4
  59.7 1.3 copy-start.6
  59.8 1.3 copy-start.7
  59.8 1.3 copy-start.8
  61.1 13.3 %copy-start.5 = (f32[6,480]{1,0:T(8,128)S(1)}, f32[6,480]{1,0:T(8,128)}, u32[]{:S(2)}) copy-start(f32[6,480]{1,0:T(8,128)} %param.11) | copy-start | bytes 34564
  75.3 21.5 %collective-permute-start.8 = (bf16[128,6,480]{0,2,1:T(8,128)(2,1)}, bf16[128,6,480]{0,2,1:T(8,128)(2,1)S(1)}, u32[]{:S(2)}, u32[]{:S(2)}) collective-permute-start(bf16[128,6,480]{0,2,1:T(8,128)(2,1)} %collective-permute-done.6), channel_id=1, source_target_pairs={{0,64},{64,128},{128,192},{192,256},{256,320},{320,384},{384,448},... | collective-permute-start | bytes 2211848 | tf_op jit(solution)/shard_map/ppermute | solution.py:96
  82.2 21.5 %collective-permute-start.9 = (bf16[128,6,480]{0,2,1:T(8,128)(2,1)}, bf16[128,6,480]{0,2,1:T(8,128)(2,1)S(1)}, u32[]{:S(2)}, u32[]{:S(2)}) collective-permute-start(bf16[128,6,480]{0,2,1:T(8,128)(2,1)} %collective-permute-done.7), channel_id=1, source_target_pairs={{64,0},{128,64},{192,128},{256,192},{320,256},{384,320},{448,384},... | collective-permute-start | bytes 2211848 | tf_op jit(solution)/shard_map/ppermute | solution.py:97
  96.8 20.3 %collective-permute-start.10 = (bf16[128,6,480]{0,2,1:T(8,128)(2,1)S(1)}, bf16[128,6,480]{0,2,1:T(8,128)(2,1)S(1)}, u32[]{:S(2)}, u32[]{:S(2)}) collective-permute-start(bf16[128,6,480]{0,2,1:T(8,128)(2,1)S(1)} %collective-permute-done.8), channel_id=1, source_target_pairs={{0,64},{64,128},{128,192},{192,256},{256,320},{320,384},{384,448},... | collective-permute-start | bytes 2211848 | tf_op jit(solution)/shard_map/ppermute | solution.py:96
  104.1 14.9 %copy-start.9 = (f32[128]{0:T(128)S(1)}, f32[128]{0:T(128)}, u32[]{:S(2)}) copy-start(f32[128]{0:T(128)} %get-tuple-element.2) | copy-start | bytes 1540
  117.6 0.8 copy-start.2
  118.4 197.2 %all-gather.2.cloned.1.call-start = ((), (), s32[]{:S(2)}) async-start(), calls=%async_computation.1 | async-start | bytes 6635520 | tf_op jit(solution)/shard_map/all_gather | solution.py:120
Sparse Core Ops, SparseCore 0:
  118.5 196.9 all-reduce.1
Sparse Core Ops, SparseCore 1:
  120.9 81.1 all-gather.1
